TPU v7x, 32 devices: a whole 2x2x4 slice. The times are simulated.
32 devices in a mesh: parts: 2 (over x), row: 16 (over z, y, core).
Axes of the slice: x: 2, y: 2, z: 4, core: 2. Of those that a mesh axis runs over, the one named last changes fastest.
Arguments:
- raw_trace: float32 [320, 768, 512], P('row', 'parts'), parts along dimension 1, may hold values from -1200 to 1200
- fir_taps: float32 [32], replicated, may hold values from -1 to 1
- templ_real: bfloat16 [32, 320, 2048], P(None, None, 'row'), may hold values from -6 to 6
- templ_imag: bfloat16 [32, 320, 2048], P(None, None, 'row'), may hold values from -6 to 6
- channel_mask: int32 [320, 2048], P(None, 'row'), may hold values 0 or 1
- moveout: int32 [320, 2048], P(None, 'row'), may hold values from 0 to 63
Outputs:
- peak: float32 [2048, 768], P('row', 'parts'), parts along dimension 1
- best: float32 [768], P('parts'), parts along dimension 0
There are 2 independent parts, one for each index of `parts`. A program takes and returns all parts, laid end to end along the dimension named above; an argument that names none is the same for every part. Nothing has to cross between parts.
All inputs are finite; a program needn't handle non-finite values. No bound on the sum of `channel_mask` on one device may be relied on, other than what follows from the above.
Results may differ from a plain program's by a relative error of at most 0.0015.
Values may be sent and summed in bfloat16 or wider, within the bound.
A program may use at most 128 MiB of HBM per device.

v0:
```python
import functools
import math

import jax
import jax.numpy as jnp
import numpy as np
from jax import lax
from jax.experimental import pallas as pl
from jax.experimental.pallas import tpu as pltpu
from jax.sharding import PartitionSpec as P

FIRST_BIN = 16

epsilon = 1e-06
VMEM_LIMIT = 60 * 1024 * 1024


def front_kernel(taps_ref, forward_ref, raw_ref, out_ref, table, rows):
    local, block, length = raw_ref.shape
    samples = length // 2
    band2 = forward_ref.shape[1]
    band = band2 // 2

    @pl.when(pl.program_id(0) == 0)
    def _():
        offsets = 2 * lax.broadcasted_iota(jnp.int32, (length, samples), 1) - lax.broadcasted_iota(
            jnp.int32, (length, samples), 0
        )
        taps = jnp.zeros((length, samples), jnp.float32)
        for k in range(taps_ref.shape[0]):
            taps = jnp.where(offsets == k, taps_ref[k], taps)
        combined = jnp.dot(
            taps, forward_ref[...], precision=lax.Precision.HIGHEST, preferred_element_type=jnp.float32
        )
        high = combined.astype(jnp.bfloat16)
        low = (combined - high.astype(jnp.float32)).astype(jnp.bfloat16)
        table[...] = jnp.concatenate([high, low], axis=1)

    weights = table[...]
    for c in range(local):
        raw = raw_ref[c]
        high = raw.astype(jnp.bfloat16)
        low = (raw - high.astype(jnp.float32)).astype(jnp.bfloat16)
        spectra = jnp.dot(high, weights, preferred_element_type=jnp.float32) + jnp.dot(
            low, weights, preferred_element_type=jnp.float32
        )
        turned = spectra.T
        value = turned[:band2] + turned[band2:]
        rows[pl.ds(c, band, stride=2 * local), :] = value[:band]
        rows[pl.ds(local + c, band, stride=2 * local), :] = value[band:]
    out_ref[0] = rows[...].astype(jnp.bfloat16)


def template_kernel(x_ref, y_ref, cos_ref, sin_ref, cos1_ref, sin1_ref, out_ref, norm_ref, cosine, sine, total):
    f = pl.program_id(0)

    @pl.when(f == 0)
    def _():
        cosine[...] = cos_ref[...]
        sine[...] = sin_ref[...]
        total[...] = jnp.zeros_like(total)

    c, s = cosine[...], sine[...]
    x = x_ref[0].astype(jnp.float32)
    y = y_ref[0].astype(jnp.float32)
    first = (x * c + y * s).astype(jnp.bfloat16)
    second = (x * s - y * c).astype(jnp.bfloat16)
    back = first.astype(jnp.float32)
    square = back * back
    total[...] += jnp.sum(square.reshape(square.shape[0] // 8, 8, square.shape[1]), axis=0)
    out_ref[0] = jnp.concatenate([first, second], axis=1).T
    c1, s1 = cos1_ref[...], sin1_ref[...]
    cosine[...] = c * c1 - s * s1
    sine[...] = s * c1 + c * s1

    @pl.when(f == pl.num_programs(0) - 1)
    def _():
        norm_ref[...] = jnp.sum(total[...], axis=0, keepdims=True)


def scan_kernel(pitch, eff_ref, spec_ref, inverse_ref, high_ref, energy_ref, cross, total):
    step = pl.program_id(0)
    count = eff_ref.shape[0]
    band = pl.num_programs(0) * count
    templates = eff_ref.shape[1] // 2

    @pl.when(step == 0)
    def _():
        total[...] = jnp.zeros_like(total)

    for i in range(count):
        spec = spec_ref[i]
        wide = spec.astype(jnp.float32)
        square = wide * wide
        total[...] += jnp.sum(square.reshape(square.shape[0] // 8, 8, square.shape[1]), axis=0)
        both = jnp.dot(eff_ref[i], spec, preferred_element_type=jnp.float32)
        f = step * count + i
        cross[pl.ds(f, templates, stride=pitch), :] = both[:templates]
        cross[pl.ds(band + f, templates, stride=pitch), :] = both[templates:]

    @pl.when(step == pl.num_programs(0) - 1)
    def _():
        energy_ref[...] = jnp.sum(total[...], axis=0, keepdims=True)
        inverse = inverse_ref[...]

        def group(j, carry):
            found = []
            for k in range(0, 8, 2):
                pair = [
                    cross[pl.ds(pl.multiple_of((j * 8 + k + q) * pitch, 8), inverse.shape[1] // 3), :] for q in range(2)
                ]
                joined = jnp.concatenate(pair, axis=1)
                high = joined.astype(jnp.bfloat16)
                low = (joined - high.astype(jnp.float32)).astype(jnp.bfloat16)
                stacked = jnp.dot(
                    inverse,
                    jnp.concatenate([high, low, high], axis=0),
                    preferred_element_type=jnp.float32,
                )
                best = jnp.max(stacked, axis=0, keepdims=True)
                found += [best[:, : best.shape[1] // 2], best[:, best.shape[1] // 2 :]]
            high_ref[pl.ds(pl.multiple_of(j * 8, 8), 8), :] = jnp.concatenate(found, axis=0)
            return carry

        lax.fori_loop(0, templates // 8, group, 0)


def best_kernel(n, mine_ref, out_ref, slots, send_sem, recv_sem):
    me = lax.axis_index("row")
    barrier = pltpu.get_barrier_semaphore()
    for step in range(1, n):
        pl.semaphore_signal(
            barrier,
            inc=1,
            device_id={"row": lax.rem(me + step, n)},
            device_id_type=pl.DeviceIdType.MESH,
        )
    pl.semaphore_wait(barrier, n - 1)
    copies = []
    for step in range(1, n):
        copy = pltpu.make_async_remote_copy(
            src_ref=mine_ref,
            dst_ref=slots.at[step - 1],
            send_sem=send_sem.at[step - 1],
            recv_sem=recv_sem.at[step - 1],
            device_id={"row": lax.rem(me + step, n)},
            device_id_type=pl.DeviceIdType.MESH,
        )
        copy.start()
        copies.append(copy)
    value = mine_ref[...]
    for step in range(1, n):
        copies[step - 1].wait()
        value = jnp.maximum(value, slots[step - 1])
    out_ref[...] = value


def best_of_row(n, value):
    return pl.pallas_call(
        functools.partial(best_kernel, n),
        out_shape=jax.ShapeDtypeStruct(value.shape, value.dtype),
        in_specs=[pl.BlockSpec(memory_space=pltpu.VMEM)],
        out_specs=pl.BlockSpec(memory_space=pltpu.VMEM),
        scratch_shapes=[
            pltpu.VMEM((n - 1,) + value.shape, value.dtype),
            pltpu.SemaphoreType.DMA((n - 1,)),
            pltpu.SemaphoreType.DMA((n - 1,)),
        ],
        compiler_params=pltpu.CompilerParams(collective_id=0, has_side_effects=True),
        name="best_of_row",
    )(value)


def body(n, raw_trace, fir_taps, templ_real, templ_imag, channel_mask, moveout):
    local, windows, length = raw_trace.shape
    samples = length // 2
    band, channels, templates = templ_real.shape
    depth = 2 * channels
    block = math.gcd(windows, 128)
    blocks = windows // block
    bins = FIRST_BIN + np.arange(band)
    lags = np.arange(samples)
    angle = 2.0 * np.pi / samples * (bins[:, None] * lags[None, :] % samples)
    inverse = np.concatenate([np.cos(angle), -np.sin(angle)], axis=0)
    forward = jnp.asarray(inverse.T, jnp.float32)
    inverse = inverse.T.astype(np.float32)
    inverse_high = jnp.asarray(inverse).astype(jnp.bfloat16)
    high_np = np.asarray(inverse.astype(jnp.bfloat16))
    inverse_low = jnp.asarray((inverse - high_np.astype(np.float32)).astype(jnp.bfloat16))
    inverse3 = jnp.concatenate([inverse_high, inverse_high, inverse_low], axis=1)

    vmem = pl.BlockSpec(memory_space=pltpu.VMEM)
    spectra = pl.pallas_call(
        front_kernel,
        grid=(blocks,),
        out_shape=jax.ShapeDtypeStruct((blocks, band * 2 * local, block), jnp.bfloat16),
        in_specs=[
            pl.BlockSpec(memory_space=pltpu.SMEM),
            vmem,
            pl.BlockSpec((local, block, length), lambda i: (0, i, 0)),
        ],
        out_specs=pl.BlockSpec((1, band * 2 * local, block), lambda i: (i, 0, 0)),
        scratch_shapes=[
            pltpu.VMEM((length, 4 * band), jnp.bfloat16),
            pltpu.VMEM((band * 2 * local, block), jnp.float32),
        ],
        compiler_params=pltpu.CompilerParams(vmem_limit_bytes=VMEM_LIMIT),
        name="front",
    )(fir_taps, forward, raw_trace)
    spectra = spectra.reshape(blocks, band, 2 * local, block)
    gathered = [lax.all_gather(spectra[i], "row", axis=1, tiled=True) for i in range(blocks)]

    def rows_of(first, second):
        shape = first.shape[:-2] + (n, local, templates)
        joined = jnp.concatenate([first.reshape(shape), second.reshape(shape)], axis=-2)
        return joined.reshape(first.shape[:-2] + (depth, templates))

    x = rows_of(templ_real, templ_imag)
    y = rows_of(templ_imag, -templ_real)
    turn = 2.0 * math.pi / samples
    first_phase = turn * (FIRST_BIN * moveout % samples).astype(jnp.float32)
    step_phase = turn * moveout.astype(jnp.float32)
    weight = channel_mask.astype(jnp.float32)
    tables = [
        weight * jnp.cos(first_phase),
        weight * jnp.sin(first_phase),
        jnp.cos(step_phase),
        jnp.sin(step_phase),
    ]
    tables = [rows_of(table, table) for table in tables]
    one = pl.BlockSpec((1, depth, templates), lambda f: (f, 0, 0))
    eff, square = pl.pallas_call(
        template_kernel,
        grid=(band,),
        out_shape=(
            jax.ShapeDtypeStruct((band, 2 * templates, depth), jnp.bfloat16),
            jax.ShapeDtypeStruct((1, templates), jnp.float32),
        ),
        in_specs=[one, one, vmem, vmem, vmem, vmem],
        out_specs=(
            pl.BlockSpec((1, 2 * templates, depth), lambda f: (f, 0, 0)),
            pl.BlockSpec((1, templates), lambda f: (0, 0)),
        ),
        scratch_shapes=[
            pltpu.VMEM((depth, templates), jnp.float32),
            pltpu.VMEM((depth, templates), jnp.float32),
            pltpu.VMEM((8, templates), jnp.float32),
        ],
        compiler_params=pltpu.CompilerParams(vmem_limit_bytes=32 * 1024 * 1024),
        cost_estimate=pl.CostEstimate(flops=40 * band * depth * templates, bytes_accessed=8 * band * depth * templates, transcendentals=0),
        name="templates",
    )(x, y, *tables)

    count = math.gcd(band, 4)
    pitch = 2 * band + 8
    highest, energy = [], []
    for i in range(blocks):
        high, squares = pl.pallas_call(
            functools.partial(scan_kernel, pitch),
            grid=(band // count,),
            out_shape=(
                jax.ShapeDtypeStruct((templates, block), jnp.float32),
                jax.ShapeDtypeStruct((1, block), jnp.float32),
            ),
            in_specs=[
                pl.BlockSpec((count, 2 * templates, depth), lambda f: (f, 0, 0)),
                pl.BlockSpec((count, depth, block), lambda f: (f, 0, 0)),
                vmem,
            ],
            out_specs=(
                pl.BlockSpec((templates, block), lambda f: (0, 0)),
                pl.BlockSpec((1, block), lambda f: (0, 0)),
            ),
            scratch_shapes=[
                pltpu.VMEM((templates * pitch, block), jnp.float32),
                pltpu.VMEM((8, block), jnp.float32),
            ],
            compiler_params=pltpu.CompilerParams(vmem_limit_bytes=32 * 1024 * 1024),
            cost_estimate=pl.CostEstimate(flops=8 * band * depth * templates * block, bytes_accessed=16 * 1024 * 1024, transcendentals=0),
            name="scan",
        )(eff, gathered[i], inverse3)
        highest.append(high)
        energy.append(squares)
    highest = jnp.concatenate(highest, axis=1)
    data_norm = jnp.sqrt(jnp.concatenate(energy, axis=1) + epsilon)
    templ_norm = jnp.sqrt(square + epsilon).reshape(templates, 1)
    scale = math.sqrt(2.0 * channels * band)
    peak = highest * scale / (templ_norm * data_norm)
    best = best_of_row(n, jnp.max(peak, axis=0).reshape(blocks, block))
    return (peak, best.reshape(windows))


def solution(mesh):
    in_specs = (
        P("row", "parts", None),
        P(),
        P(None, None, "row"),
        P(None, None, "row"),
        P(None, "row"),
        P(None, "row"),
    )
    out_specs = (P("row", "parts"), P("parts"))
    return jax.shard_map(
        functools.partial(body, mesh.shape["row"]),
        mesh=mesh,
        in_specs=in_specs,
        out_specs=out_specs,
        check_vma=False,
    )
```

profile of v0, /device:TPU:0, one launch (start us, length us, event | category | flops | bytes accessed | tf_op | source)
XLA Modules:
  0.0 226.4 jit_solution(18009841217907255241)
XLA Ops:
  7.2 0.0 copy-start.10
  7.2 0.0 all-gather.4.cloned.1.call-start
  7.2 11.1 %front.1 = bf16[3,1280,128]{2,1,0:T(8,128)(2,1)} custom-call(f32[32]{0:T(128)} %taps_ref.1, f32[256,64]{1,0:T(8,128)} %constant.30.clone.forward_ref, f32[20,384,512]{2,1,0:T(8,128)} %raw_ref.1), custom_call_target="tpu_custom_call" | custom-call | tf_op jit(solution)/shard_map/front/pallas_call | solution.py:193
  18.3 2.2 fusion.9
  20.5 0.0 all-gather.4.cloned.1.call-update
  20.5 0.0 all-gather.6.cloned.1.call-start
  20.5 0.7 all-gather.6.cloned.1.call-update
  21.2 0.0 all-gather.8.cloned.1.call-start
  21.3 0.7 all-gather.8.cloned.1.call-update
  22.0 0.0 copy-done.10
  22.0 0.0 copy-start.11
  22.0 1.7 copy.12
  23.7 0.0 copy-done.11
  23.7 1.9 copy_negate_fusion
  25.7 2.6 %pad_maximum_fusion.1 = (bf16[32,16,40,128]{3,0,2,1:T(8,128)(2,1)S(1)}, bf16[32,16,40,128]{3,0,2,1:T(8,128)(2,1)S(1)}) fusion(bf16[32,16,20,128]{3,0,2,1:T(8,128)(2,1)S(1)} %bitcast.29, bf16[32,16,20,128]{3,0,2,1:T(8,128)(2,1)S(1)} %bitcast.28, bf16[32,16,20,128]{3,0,2,1:T(8,128)(2,1)S(1)} %bitcast.30), kind=kLoop, calls=%fused_computation.1 | loop fusion | flops 5242880 | bytes 18350080 | tf_op jit(solution)/shard_map/concatenate | solution.py:215
  28.2 4.4 %copy.13 = bf16[32,16,40,128]{3,2,1,0:T(8,128)(2,1)} copy(bf16[32,16,40,128]{3,0,2,1:T(8,128)(2,1)S(1)} %get-tuple-element.21) | data formatting | bytes 10485760 | tf_op jit(solution)/shard_map/concatenate | solution.py:215
  32.6 0.0 copy-start.12
  32.6 0.0 copy-start.13
  32.6 4.4 %copy.15 = bf16[32,16,40,128]{3,2,1,0:T(8,128)(2,1)} copy(bf16[32,16,40,128]{3,0,2,1:T(8,128)(2,1)S(1)} %get-tuple-element.20) | data formatting | bytes 10485760 | tf_op jit(solution)/shard_map/concatenate | solution.py:215
  37.0 0.0 copy-done.12
  37.0 0.0 copy-done.13
  37.0 1.3 sine_multiply_fusion
  38.5 0.0 copy-start.4
  38.5 2.5 %copy-done.4 = bf16[32,16,40,128]{3,2,1,0:T(8,128)(2,1)S(1)} copy-done((bf16[32,16,40,128]{3,2,1,0:T(8,128)(2,1)S(1)}, bf16[32,16,40,128]{3,2,1,0:T(8,128)(2,1)}, u32[]{:S(2)}) %copy-start.4) | copy-done | bytes 5242904
  41.0 0.0 copy-start.5
  41.0 2.5 %copy-done.5 = bf16[32,16,40,128]{3,2,1,0:T(8,128)(2,1)S(1)} copy-done((bf16[32,16,40,128]{3,2,1,0:T(8,128)(2,1)S(1)}, bf16[32,16,40,128]{3,2,1,0:T(8,128)(2,1)}, u32[]{:S(2)}) %copy-start.5) | copy-done | bytes 5242904
  43.5 0.0 copy-start.9
  43.5 8.6 %templates.1 = (bf16[32,256,640]{2,1,0:T(8,128)(2,1)S(1)}, f32[1,128]{1,0:T(1,128)S(1)}) custom-call(bf16[32,640,128]{2,1,0:T(8,128)(2,1)S(1)} %bitcast.19, bf16[32,640,128]{2,1,0:T(8,128)(2,1)S(1)} %bitcast.20, f32[640,128]{1,0:T(8,128)S(1)} %bitcast.21, f32[640,128]{1,0:T(8,128)S(1)} %bitcast.22, f32[640,128]{1,0:T(8,128)S(1)} %bitcast.23, ...), custom_call_target="tpu_custom_call" | custom-call | flops 104857600 | bytes 20971520 | tf_op jit(solution)/shard_map/templates/pallas_call | solution.py:232
  52.1 0.0 copy-start
  52.1 4.0 %copy-done = bf16[32,256,640]{2,1,0:T(8,128)(2,1)} copy-done((bf16[32,256,640]{2,1,0:T(8,128)(2,1)}, bf16[32,256,640]{2,1,0:T(8,128)(2,1)S(1)}, u32[]{:S(2)}) %copy-start) | copy-done | bytes 10485784
  56.1 23.4 %all-gather.4.cloned.1.call-done.spec_ref = bf16[32,640,128]{2,1,0:T(8,128)(2,1)} async-done(((bf16[32,40,128]{2,1,0:T(8,128)(2,1)}), bf16[32,640,128]{2,1,0:T(8,128)(2,1)}) %all-gather.4.cloned.1.call-update) | async-done | bytes 5242896 | tf_op jit(solution)/shard_map/all_gather | solution.py:211
  79.5 0.0 copy-done.9
  79.5 0.0 copy-start.1
  79.5 4.0 %copy-done.1 = bf16[32,256,640]{2,1,0:T(8,128)(2,1)S(1)} copy-done((bf16[32,256,640]{2,1,0:T(8,128)(2,1)S(1)}, bf16[32,256,640]{2,1,0:T(8,128)(2,1)}, u32[]{:S(2)}) %copy-start.1) | copy-done | bytes 10485784
  83.5 0.0 copy-start.6
  83.5 2.5 %copy-done.6 = bf16[32,640,128]{2,1,0:T(8,128)(2,1)S(1)} copy-done((bf16[32,640,128]{2,1,0:T(8,128)(2,1)S(1)}, bf16[32,640,128]{2,1,0:T(8,128)(2,1)}, u32[]{:S(2)}) %copy-start.6) | copy-done | bytes 5242904
  86.0 9.2 %scan.3 = (f32[128,128]{1,0:T(8,128)S(1)}, f32[1,128]{1,0:T(1,128)S(1)}) custom-call(bf16[32,256,640]{2,1,0:T(8,128)(2,1)S(1)} %copy-done.1, bf16[32,640,128]{2,1,0:T(8,128)(2,1)S(1)} %copy-done.6, bf16[256,192]{1,0:T(8,128)(2,1)S(1)} %copy-done.9), custom_call_target="tpu_custom_call" | custom-call | flops 2684354560 | bytes 16777216 | tf_op jit(solution)/shard_map/scan/pallas_call | solution.py:258
  95.2 41.4 %all-gather.6.cloned.1.call-done.spec_ref = bf16[32,640,128]{2,1,0:T(8,128)(2,1)} async-done(((bf16[32,40,128]{2,1,0:T(8,128)(2,1)}), bf16[32,640,128]{2,1,0:T(8,128)(2,1)}) %all-gather.6.cloned.1.call-update) | async-done | bytes 5242896 | tf_op jit(solution)/shard_map/all_gather | solution.py:211
  136.6 4.0 %copy-done.2 = bf16[32,256,640]{2,1,0:T(8,128)(2,1)S(1)} copy-done((bf16[32,256,640]{2,1,0:T(8,128)(2,1)S(1)}, bf16[32,256,640]{2,1,0:T(8,128)(2,1)}, u32[]{:S(2)}) %copy-start.2) | copy-done | bytes 10485784
  140.6 2.5 %copy-done.7 = bf16[32,640,128]{2,1,0:T(8,128)(2,1)S(1)} copy-done((bf16[32,640,128]{2,1,0:T(8,128)(2,1)S(1)}, bf16[32,640,128]{2,1,0:T(8,128)(2,1)}, u32[]{:S(2)}) %copy-start.7) | copy-done | bytes 5242904
  143.1 9.2 %scan.4 = (f32[128,128]{1,0:T(8,128)S(1)}, f32[1,128]{1,0:T(1,128)S(1)}) custom-call(bf16[32,256,640]{2,1,0:T(8,128)(2,1)S(1)} %copy-done.2, bf16[32,640,128]{2,1,0:T(8,128)(2,1)S(1)} %copy-done.7, bf16[256,192]{1,0:T(8,128)(2,1)S(1)} %copy-done.9), custom_call_target="tpu_custom_call" | custom-call | flops 2684354560 | bytes 16777216 | tf_op jit(solution)/shard_map/scan/pallas_call | solution.py:258
  152.3 41.3 %all-gather.8.cloned.1.call-done.spec_ref = bf16[32,640,128]{2,1,0:T(8,128)(2,1)} async-done(((bf16[32,40,128]{2,1,0:T(8,128)(2,1)}), bf16[32,640,128]{2,1,0:T(8,128)(2,1)}) %all-gather.8.cloned.1.call-update) | async-done | bytes 5242896 | tf_op jit(solution)/shard_map/all_gather | solution.py:211
  193.6 4.0 %copy-done.3 = bf16[32,256,640]{2,1,0:T(8,128)(2,1)S(1)} copy-done((bf16[32,256,640]{2,1,0:T(8,128)(2,1)S(1)}, bf16[32,256,640]{2,1,0:T(8,128)(2,1)}, u32[]{:S(2)}) %copy-start.3) | copy-done | bytes 10485784
  197.6 2.5 %copy-done.8 = bf16[32,640,128]{2,1,0:T(8,128)(2,1)S(1)} copy-done((bf16[32,640,128]{2,1,0:T(8,128)(2,1)S(1)}, bf16[32,640,128]{2,1,0:T(8,128)(2,1)}, u32[]{:S(2)}) %copy-start.8) | copy-done | bytes 5242904
  200.1 9.2 %scan.5 = (f32[128,128]{1,0:T(8,128)S(1)}, f32[1,128]{1,0:T(1,128)S(1)}) custom-call(bf16[32,256,640]{2,1,0:T(8,128)(2,1)S(1)} %copy-done.3, bf16[32,640,128]{2,1,0:T(8,128)(2,1)S(1)} %copy-done.8, bf16[256,192]{1,0:T(8,128)(2,1)S(1)} %copy-done.9), custom_call_target="tpu_custom_call" | custom-call | flops 2684354560 | bytes 16777216 | tf_op jit(solution)/shard_map/scan/pallas_call | solution.py:258
  209.3 1.4 fusion.7
  210.7 7.9 %best_of_row.1 = f32[3,128]{1,0:T(4,128)} custom-call(f32[3,128]{1,0:T(4,128)} %bitcast.34), custom_call_target="tpu_custom_call" | custom-call | tf_op jit(solution)/shard_map/best_of_row/pallas_call | solution.py:159
  218.6 1.2 copy.19
  (14 shorter events, 0.2 us)
Async XLA Ops:
  7.2 14.8 %copy-start.10 = (bf16[32,320,128]{2,1,0:T(8,128)(2,1)S(1)}, bf16[32,320,128]{2,1,0:T(8,128)(2,1)}, u32[]{:S(2)}) copy-start(bf16[32,320,128]{2,1,0:T(8,128)(2,1)} %param.12) | copy-start | bytes 7864324
  7.2 72.4 %all-gather.4.cloned.1.call-start = ((), (), s32[]{:S(2)}) async-start(), calls=%async_computation | async-start | bytes 5570560 | tf_op jit(solution)/shard_map/all_gather | solution.py:211
  20.5 116.1 %all-gather.6.cloned.1.call-start = ((), (), s32[]{:S(2)}) async-start(), calls=%async_computation.1 | async-start | bytes 5570560 | tf_op jit(solution)/shard_map/all_gather | solution.py:211
  21.2 172.4 %all-gather.8.cloned.1.call-start = ((), (), s32[]{:S(2)}) async-start(), calls=%async_computation.2 | async-start | bytes 5570560 | tf_op jit(solution)/shard_map/all_gather | solution.py:211
  22.0 1.7 copy-start.11
  32.6 4.4 %copy-start.12 = (s32[320,128]{1,0:T(8,128)S(1)}, s32[320,128]{1,0:T(8,128)}, u32[]{:S(2)}) copy-start(s32[320,128]{1,0:T(8,128)} %param.13) | copy-start | bytes 491524
  32.6 4.4 %copy-start.13 = (s32[320,128]{1,0:T(8,128)S(1)}, s32[320,128]{1,0:T(8,128)}, u32[]{:S(2)}) copy-start(s32[320,128]{1,0:T(8,128)} %param.14) | copy-start | bytes 491524
  38.5 2.5 %copy-start.4 = (bf16[32,16,40,128]{3,2,1,0:T(8,128)(2,1)S(1)}, bf16[32,16,40,128]{3,2,1,0:T(8,128)(2,1)}, u32[]{:S(2)}) copy-start(bf16[32,16,40,128]{3,2,1,0:T(8,128)(2,1)} %copy.13) | copy-start | bytes 15728644
  41.0 2.5 %copy-start.5 = (bf16[32,16,40,128]{3,2,1,0:T(8,128)(2,1)S(1)}, bf16[32,16,40,128]{3,2,1,0:T(8,128)(2,1)}, u32[]{:S(2)}) copy-start(bf16[32,16,40,128]{3,2,1,0:T(8,128)(2,1)} %copy.15) | copy-start | bytes 15728644
  43.5 36.0 %copy-start.9 = (bf16[256,192]{1,0:T(8,128)(2,1)S(1)}, bf16[256,192]{1,0:T(8,128)(2,1)}, u32[]{:S(2)}) copy-start(bf16[256,192]{1,0:T(8,128)(2,1)} %constant.34.inverse_ref) | copy-start | bytes 294916
  52.1 4.0 %copy-start = (bf16[32,256,640]{2,1,0:T(8,128)(2,1)}, bf16[32,256,640]{2,1,0:T(8,128)(2,1)S(1)}, u32[]{:S(2)}) copy-start(bf16[32,256,640]{2,1,0:T(8,128)(2,1)S(1)} %get-tuple-element.10.eff_ref) | copy-start | bytes 31457284
  79.5 4.0 %copy-start.1 = (bf16[32,256,640]{2,1,0:T(8,128)(2,1)S(1)}, bf16[32,256,640]{2,1,0:T(8,128)(2,1)}, u32[]{:S(2)}) copy-start(bf16[32,256,640]{2,1,0:T(8,128)(2,1)} %copy-done) | copy-start | bytes 31457284
  83.5 2.5 %copy-start.6 = (bf16[32,640,128]{2,1,0:T(8,128)(2,1)S(1)}, bf16[32,640,128]{2,1,0:T(8,128)(2,1)}, u32[]{:S(2)}) copy-start(bf16[32,640,128]{2,1,0:T(8,128)(2,1)} %all-gather.4.cloned.1.call-done.spec_ref) | copy-start | bytes 15728644
  136.6 4.0 %copy-start.2 = (bf16[32,256,640]{2,1,0:T(8,128)(2,1)S(1)}, bf16[32,256,640]{2,1,0:T(8,128)(2,1)}, u32[]{:S(2)}) copy-start(bf16[32,256,640]{2,1,0:T(8,128)(2,1)} %copy-done) | copy-start | bytes 31457284
  140.6 2.5 %copy-start.7 = (bf16[32,640,128]{2,1,0:T(8,128)(2,1)S(1)}, bf16[32,640,128]{2,1,0:T(8,128)(2,1)}, u32[]{:S(2)}) copy-start(bf16[32,640,128]{2,1,0:T(8,128)(2,1)} %all-gather.6.cloned.1.call-done.spec_ref) | copy-start | bytes 15728644
  193.6 4.0 %copy-start.3 = (bf16[32,256,640]{2,1,0:T(8,128)(2,1)S(1)}, bf16[32,256,640]{2,1,0:T(8,128)(2,1)}, u32[]{:S(2)}) copy-start(bf16[32,256,640]{2,1,0:T(8,128)(2,1)} %copy-done) | copy-start | bytes 31457284
  197.6 2.5 %copy-start.8 = (bf16[32,640,128]{2,1,0:T(8,128)(2,1)S(1)}, bf16[32,640,128]{2,1,0:T(8,128)(2,1)}, u32[]{:S(2)}) copy-start(bf16[32,640,128]{2,1,0:T(8,128)(2,1)} %all-gather.8.cloned.1.call-done.spec_ref) | copy-start | bytes 15728644
Sparse Core Ops, SparseCore 0:
  20.6 58.8 all-gather.3
  81.7 54.8 all-gather.5
  138.8 54.7 all-gather.7
where the time goes:
time: 227 us; the launch traced here: 226 us
  waiting for transfers between devices  108 us (48%)
  Pallas kernels  55.2 us (24%)
  local copies, waits for them, and re-layouts  42.3 us (19%)
  between operations  13.9 us (6%)
  other arithmetic  7.26 us (3%)
    all_gather x3, waiting for transfers between devices, body(): lax.all_gather(spectra[i], 'row', axis=1, tiled=True)  106 us
    unnamed x30, local copies, waits for them, and re-layouts  31.4 us
    pallas_call x3, Pallas kernels, body(): pl.pallas_call(functools.partial(scan_kernel, pitch), grid=(band // count...  27.6 us
    pallas_call x1, Pallas kernels, body(): pl.pallas_call(front_kernel, grid=(blocks,), out_shape=jax.ShapeDtypeStru...  11.1 us
    concatenate x2, local copies, waits for them, and re-layouts, rows_of(): jnp.concatenate([first.reshape(shape), second.reshape(shape)], axis=-2)  8.74 us
    pallas_call x1, Pallas kernels, body(): pl.pallas_call(template_kernel, grid=(band,), out_shape=(jax.ShapeDtypeSt...  8.57 us
    pallas_call x1, Pallas kernels, best_of_row(): pl.pallas_call(functools.partial(best_kernel, n), out_shape=jax.ShapeDtyp...  7.91 us
  transfers between devices with their start and end apart: 3, of which 3 were waited for; matrix products, arithmetic and copies ran while one was open for 7% of the time, Pallas kernels for 12%

commit v1 on v0

--- a/solution.py
+++ b/solution.py
@@ -20,6 +20,7 @@
     samples = length // 2
     band2 = forward_ref.shape[1]
     band = band2 // 2
+    held = rows.shape[0] // band
 
     @pl.when(pl.program_id(0) == 0)
     def _():
@@ -35,6 +36,8 @@
         high = combined.astype(jnp.bfloat16)
         low = (combined - high.astype(jnp.float32)).astype(jnp.bfloat16)
         table[...] = jnp.concatenate([high, low], axis=1)
+        if held > 2 * local:
+            rows[...] = jnp.zeros_like(rows)
 
     weights = table[...]
     for c in range(local):
@@ -46,8 +49,8 @@
         )
         turned = spectra.T
         value = turned[:band2] + turned[band2:]
-        rows[pl.ds(c, band, stride=2 * local), :] = value[:band]
-        rows[pl.ds(local + c, band, stride=2 * local), :] = value[band:]
+        rows[pl.ds(c, band, stride=held), :] = value[:band]
+        rows[pl.ds(local + c, band, stride=held), :] = value[band:]
     out_ref[0] = rows[...].astype(jnp.bfloat16)
 
 
@@ -78,36 +81,107 @@
         norm_ref[...] = jnp.sum(total[...], axis=0, keepdims=True)
 
 
-def scan_kernel(pitch, eff_ref, spec_ref, inverse_ref, high_ref, energy_ref, cross, total):
-    step = pl.program_id(0)
-    count = eff_ref.shape[0]
-    band = pl.num_programs(0) * count
+def scan_kernel(n, pitch, count, eff_ref, inverse_ref, spec_ref, high_ref, energy_ref, gathered, buffer, cross, total, send_sem, recv_sem, own_sem, load_sem):
+    blocks, band, held, block = spec_ref.shape
     templates = eff_ref.shape[1] // 2
-
-    @pl.when(step == 0)
-    def _():
+    layers = n // 4
+    me = lax.axis_index("row")
+    z, y, core = me // 4, lax.rem(me // 2, 2), lax.rem(me, 2)
+
+    def index(z, y, core):
+        return z * 4 + y * 2 + core
+
+    def place(i, origin):
+        return gathered.at[i, :, pl.ds(pl.multiple_of(origin * held, 8), held), :]
+
+    def send(i, origin, target, kind, own=False):
+        return pltpu.make_async_remote_copy(
+            src_ref=spec_ref.at[i] if own else place(i, origin),
+            dst_ref=place(i, origin),
+            send_sem=send_sem.at[kind, i],
+            recv_sem=recv_sem.at[i, origin],
+            device_id={"row": target},
+            device_id_type=pl.DeviceIdType.MESH,
+        )
+
+    def arrived(i, origin):
+        send(i, origin, index(z, y, 1 - core), 0).wait_recv()
+
+    across = index(z, 1 - y, core)
+    partner = index(z, y, 1 - core)
+    barrier = pltpu.get_barrier_semaphore()
+    targets = [index(lax.rem(z + s, layers), y, core) for s in range(1, layers)]
+    for target in targets + [across, partner]:
+        pl.semaphore_signal(barrier, inc=1, device_id={"row": target}, device_id_type=pl.DeviceIdType.MESH)
+    pl.semaphore_wait(barrier, layers + 1)
+
+    sends = []
+
+    def start(i, origin, target, kind, own=False):
+        copy = send(i, origin, target, kind, own)
+        copy.start()
+        sends.append(copy)
+
+    own = [pltpu.make_async_copy(spec_ref.at[i], place(i, me), own_sem.at[i]) for i in range(blocks)]
+    for i in range(blocks):
+        start(i, me, across, 0, True)
+        for s in range(1, layers):
+            start(i, me, targets[s - 1], 2 * n + s, True)
+        start(i, me, partner, n, True)
+        own[i].start()
+
+    def along(i):
+        for s in range(1, layers):
+            origin = index(lax.rem(z + s, layers), y, core)
+            arrived(i, origin)
+            start(i, origin, across, s, False)
+            start(i, origin, partner, n + s, False)
+
+    def over(i):
+        for s in range(layers):
+            origin = index(lax.rem(z + s, layers), 1 - y, core)
+            arrived(i, origin)
+            start(i, origin, partner, n + layers + s, False)
+
+    def beside(i):
+        for s in range(layers):
+            for side in (y, 1 - y):
+                arrived(i, index(lax.rem(z + s, layers), side, 1 - core))
+
+    inverse = inverse_ref[...]
+
+    def scan(i):
+        own[i].wait()
+        loads = [
+            pltpu.make_async_copy(
+                gathered.at[i, pl.ds(g * count, count)], buffer.at[pl.ds(g * count, count)], load_sem.at[g]
+            )
+            for g in range(band // count)
+        ]
+        for load in loads:
+            load.start()
         total[...] = jnp.zeros_like(total)
-
-    for i in range(count):
-        spec = spec_ref[i]
-        wide = spec.astype(jnp.float32)
-        square = wide * wide
-        total[...] += jnp.sum(square.reshape(square.shape[0] // 8, 8, square.shape[1]), axis=0)
-        both = jnp.dot(eff_ref[i], spec, preferred_element_type=jnp.float32)
-        f = step * count + i
-        cross[pl.ds(f, templates, stride=pitch), :] = both[:templates]
-        cross[pl.ds(band + f, templates, stride=pitch), :] = both[templates:]
-
-    @pl.when(step == pl.num_programs(0) - 1)
-    def _():
-        energy_ref[...] = jnp.sum(total[...], axis=0, keepdims=True)
-        inverse = inverse_ref[...]
+        for g, load in enumerate(loads):
+            load.wait()
+
+            def one(f, carry):
+                spec = buffer[f]
+                wide = spec.astype(jnp.float32)
+                square = wide * wide
+                total[...] += jnp.sum(square.reshape(square.shape[0] // 8, 8, square.shape[1]), axis=0)
+                both = jnp.dot(eff_ref[f], spec, preferred_element_type=jnp.float32)
+                cross[pl.ds(f, templates, stride=pitch), :] = both[:templates]
+                cross[pl.ds(band + f, templates, stride=pitch), :] = both[templates:]
+                return carry
+
+            lax.fori_loop(g * count, (g + 1) * count, one, 0)
+        energy_ref[i] = jnp.sum(total[...], axis=0, keepdims=True)
 
         def group(j, carry):
             found = []
             for k in range(0, 8, 2):
                 pair = [
-                    cross[pl.ds(pl.multiple_of((j * 8 + k + q) * pitch, 8), inverse.shape[1] // 3), :] for q in range(2)
+                    cross[pl.ds(pl.multiple_of((j * 8 + k + q) * pitch, 8), 2 * band), :] for q in range(2)
                 ]
                 joined = jnp.concatenate(pair, axis=1)
                 high = joined.astype(jnp.bfloat16)
@@ -118,11 +192,23 @@
                     preferred_element_type=jnp.float32,
                 )
                 best = jnp.max(stacked, axis=0, keepdims=True)
-                found += [best[:, : best.shape[1] // 2], best[:, best.shape[1] // 2 :]]
-            high_ref[pl.ds(pl.multiple_of(j * 8, 8), 8), :] = jnp.concatenate(found, axis=0)
+                found += [best[:, :block], best[:, block:]]
+            high_ref[pl.ds(pl.multiple_of(j * 8, 8), 8), i * block : (i + 1) * block] = jnp.concatenate(found, axis=0)
             return carry
 
         lax.fori_loop(0, templates // 8, group, 0)
+
+    along(0)
+    over(0)
+    for i in range(blocks):
+        if i + 1 < blocks:
+            along(i + 1)
+        beside(i)
+        scan(i)
+        if i + 1 < blocks:
+            over(i + 1)
+    for copy in sends:
+        copy.wait_send()
 
 
 def best_kernel(n, mine_ref, out_ref, slots, send_sem, recv_sem):
@@ -175,7 +261,8 @@
     local, windows, length = raw_trace.shape
     samples = length // 2
     band, channels, templates = templ_real.shape
-    depth = 2 * channels
+    held = -(-2 * local // 8) * 8
+    depth = n * held
     block = math.gcd(windows, 128)
     blocks = windows // block
     bins = FIRST_BIN + np.arange(band)
@@ -193,26 +280,27 @@
     spectra = pl.pallas_call(
         front_kernel,
         grid=(blocks,),
-        out_shape=jax.ShapeDtypeStruct((blocks, band * 2 * local, block), jnp.bfloat16),
+        out_shape=jax.ShapeDtypeStruct((blocks, band * held, block), jnp.bfloat16),
         in_specs=[
             pl.BlockSpec(memory_space=pltpu.SMEM),
             vmem,
             pl.BlockSpec((local, block, length), lambda i: (0, i, 0)),
         ],
-        out_specs=pl.BlockSpec((1, band * 2 * local, block), lambda i: (i, 0, 0)),
+        out_specs=pl.BlockSpec((1, band * held, block), lambda i: (i, 0, 0)),
         scratch_shapes=[
             pltpu.VMEM((length, 4 * band), jnp.bfloat16),
-            pltpu.VMEM((band * 2 * local, block), jnp.float32),
+            pltpu.VMEM((band * held, block), jnp.float32),
         ],
         compiler_params=pltpu.CompilerParams(vmem_limit_bytes=VMEM_LIMIT),
         name="front",
     )(fir_taps, forward, raw_trace)
-    spectra = spectra.reshape(blocks, band, 2 * local, block)
-    gathered = [lax.all_gather(spectra[i], "row", axis=1, tiled=True) for i in range(blocks)]
+    spectra = spectra.reshape(blocks, band, held, block)
 
     def rows_of(first, second):
         shape = first.shape[:-2] + (n, local, templates)
         joined = jnp.concatenate([first.reshape(shape), second.reshape(shape)], axis=-2)
+        if held > 2 * local:
+            joined = jnp.pad(joined, [(0, 0)] * (joined.ndim - 2) + [(0, held - 2 * local), (0, 0)])
         return joined.reshape(first.shape[:-2] + (depth, templates))
 
     x = rows_of(templ_real, templ_imag)
@@ -253,36 +341,31 @@
 
     count = math.gcd(band, 4)
     pitch = 2 * band + 8
-    highest, energy = [], []
-    for i in range(blocks):
-        high, squares = pl.pallas_call(
-            functools.partial(scan_kernel, pitch),
-            grid=(band // count,),
-            out_shape=(
-                jax.ShapeDtypeStruct((templates, block), jnp.float32),
-                jax.ShapeDtypeStruct((1, block), jnp.float32),
-            ),
-            in_specs=[
-                pl.BlockSpec((count, 2 * templates, depth), lambda f: (f, 0, 0)),
-                pl.BlockSpec((count, depth, block), lambda f: (f, 0, 0)),
-                vmem,
-            ],
-            out_specs=(
-                pl.BlockSpec((templates, block), lambda f: (0, 0)),
-                pl.BlockSpec((1, block), lambda f: (0, 0)),
-            ),
-            scratch_shapes=[
-                pltpu.VMEM((templates * pitch, block), jnp.float32),
-                pltpu.VMEM((8, block), jnp.float32),
-            ],
-            compiler_params=pltpu.CompilerParams(vmem_limit_bytes=32 * 1024 * 1024),
-            cost_estimate=pl.CostEstimate(flops=8 * band * depth * templates * block, bytes_accessed=16 * 1024 * 1024, transcendentals=0),
-            name="scan",
-        )(eff, gathered[i], inverse3)
-        highest.append(high)
-        energy.append(squares)
-    highest = jnp.concatenate(highest, axis=1)
-    data_norm = jnp.sqrt(jnp.concatenate(energy, axis=1) + epsilon)
+    anywhere = pl.BlockSpec(memory_space=pl.ANY)
+    highest, energy, _ = pl.pallas_call(
+        functools.partial(scan_kernel, n, pitch, count),
+        out_shape=(
+            jax.ShapeDtypeStruct((templates, windows), jnp.float32),
+            jax.ShapeDtypeStruct((blocks, 1, block), jnp.float32),
+            jax.ShapeDtypeStruct((blocks, band, depth, block), jnp.bfloat16),
+        ),
+        in_specs=[vmem, vmem, anywhere],
+        out_specs=(vmem, vmem, anywhere),
+        scratch_shapes=[
+            pltpu.VMEM((band, depth, block), jnp.bfloat16),
+            pltpu.VMEM((templates * pitch, block), jnp.float32),
+            pltpu.VMEM((8, block), jnp.float32),
+            pltpu.SemaphoreType.DMA((3 * n, blocks)),
+            pltpu.SemaphoreType.DMA((blocks, n)),
+            pltpu.SemaphoreType.DMA((blocks,)),
+            pltpu.SemaphoreType.DMA((band // count,)),
+        ],
+        compiler_params=pltpu.CompilerParams(
+            collective_id=1, has_side_effects=True, vmem_limit_bytes=VMEM_LIMIT
+        ),
+        name="gather_scan",
+    )(eff, inverse3, spectra)
+    data_norm = jnp.sqrt(energy.reshape(1, windows) + epsilon)
     templ_norm = jnp.sqrt(square + epsilon).reshape(templates, 1)
     scale = math.sqrt(2.0 * channels * band)
     peak = highest * scale / (templ_norm * data_norm)

time: 227 us -> 193 us (0.85)
  Pallas kernels: 55.2 us -> 170 us
  waiting for transfers between devices: 108 us -> 0 us
  local copies, waits for them, and re-layouts: 42.3 us -> 11 us
  between operations: 13.9 us -> 0.78 us
  other arithmetic: 7.26 us -> 11.3 us
    all_gather x3 -> x0, waiting for transfers between devices: 106 us -> none  [body(): lax.all_gather(spectra[i], 'row', axis=1, tiled=True)]
    pallas_call x3 -> x1, Pallas kernels: 27.6 us -> 128 us  [body(): pl.pallas_call(functools.partial(scan_kernel, n, pitch, count), out_shape...]
    unnamed x30 -> x12, local copies, waits for them, and re-layouts: 31.4 us -> 6.93 us
    pallas_call x1, Pallas kernels: 7.91 us -> 22.8 us  [best_of_row(): pl.pallas_call(functools.partial(best_kernel, n), out_shape=jax.ShapeDtyp...]
    concatenate x2, local copies, waits for them, and re-layouts: 8.74 us -> 4.05 us  [rows_of(): jnp.concatenate([first.reshape(shape), second.reshape(shape)], axis=-2)]
  transfers between devices with their start and end apart: 3 -> 0, of which waited for: 3 -> 0; matrix products, arithmetic and copies ran while one was open for 7% -> 0% of each run, Pallas kernels for 12% -> 0%
where the time goes in v1:
time: 193 us
  Pallas kernels  170 us (88%)
  other arithmetic  11.3 us (6%)
  local copies, waits for them, and re-layouts  11 us (6%)
    pallas_call x1, Pallas kernels, body(): pl.pallas_call(functools.partial(scan_kernel, n, pitch, count), out_shape...  128 us
    pallas_call x1, Pallas kernels, best_of_row(): pl.pallas_call(functools.partial(best_kernel, n), out_shape=jax.ShapeDtyp...  22.8 us
    pallas_call x1, Pallas kernels, body(): pl.pallas_call(front_kernel, grid=(blocks,), out_shape=jax.ShapeDtypeStru...  11 us
    pallas_call x1, Pallas kernels, body(): pl.pallas_call(template_kernel, grid=(band,), out_shape=(jax.ShapeDtypeSt...  8.59 us
    unnamed x12, local copies, waits for them, and re-layouts  6.93 us
    concatenate x5, other arithmetic, rows_of(): jnp.concatenate([first.reshape(shape), second.reshape(shape)], axis=-2)  4.12 us
    concatenate x2, local copies, waits for them, and re-layouts, rows_of(): jnp.concatenate([first.reshape(shape), second.reshape(shape)], axis=-2)  4.05 us

profile of v1, /device:TPU:0, one launch (start us, length us, event | category | flops | bytes accessed | tf_op | source)
XLA Modules:
  0.0 193.1 jit_solution(12027215327901104250)
XLA Ops:
  0.6 2.3 %sine_multiply_fusion = (f32[320,128]{1,0:T(8,128)S(1)}, f32[320,128]{1,0:T(8,128)S(1)}, f32[320,128]{1,0:T(8,128)S(1)}, f32[320,128]{1,0:T(8,128)S(1)}) fusion(s32[320,128]{1,0:T(8,128)} %param.13, s32[320,128]{1,0:T(8,128)} %param.14), kind=kLoop, calls=%fused_computation.14 | loop fusion | flops 778240 | bytes 983040 | tf_op jit(solution)/shard_map/mul | solution.py:314
  3.0 0.7 pad_maximum_fusion.5
  3.8 0.7 pad_maximum_fusion.4
  4.5 0.0 copy-start.3
  4.5 11.0 %front.1 = bf16[3,1280,128]{2,1,0:T(8,128)(2,1)} custom-call(f32[32]{0:T(128)} %taps_ref.1, f32[256,64]{1,0:T(8,128)} %constant.30.clone.forward_ref, f32[20,384,512]{2,1,0:T(8,128)} %raw_ref.1), custom_call_target="tpu_custom_call" | custom-call | tf_op jit(solution)/shard_map/front/pallas_call | solution.py:280
  15.6 0.0 copy-start.4
  15.6 0.0 copy-done.3
  15.6 1.7 copy.12
  17.3 0.0 copy-done.4
  17.3 1.9 %copy_negate_fusion = (bf16[32,320,128]{2,0,1:T(8,128)(2,1)S(1)}, bf16[32,320,128]{2,0,1:T(8,128)(2,1)S(1)}) fusion(bf16[32,320,128]{2,1,0:T(8,128)(2,1)S(1)} %copy-done.4), kind=kLoop, calls=%fused_computation.20 | loop fusion | flops 1310720 | bytes 7864320 | tf_op jit(solution)/shard_map/neg | solution.py:307
  19.2 2.6 %pad_maximum_fusion.1 = (bf16[32,16,40,128]{3,0,2,1:T(8,128)(2,1)S(1)}, bf16[32,16,40,128]{3,0,2,1:T(8,128)(2,1)S(1)}) fusion(bf16[32,16,20,128]{3,0,2,1:T(8,128)(2,1)S(1)} %bitcast.22, bf16[32,16,20,128]{3,0,2,1:T(8,128)(2,1)S(1)} %bitcast.21, bf16[32,16,20,128]{3,0,2,1:T(8,128)(2,1)S(1)} %bitcast.23), kind=kLoop, calls=%fused_computation.1 | loop fusion | flops 5242880 | bytes 18350080 | tf_op jit(solution)/shard_map/concatenate | solution.py:301
  21.8 2.0 %copy.15 = bf16[32,16,40,128]{3,2,1,0:T(8,128)(2,1)S(1)} copy(bf16[32,16,40,128]{3,0,2,1:T(8,128)(2,1)S(1)} %get-tuple-element.12) | data formatting | bytes 10485760 | tf_op jit(solution)/shard_map/concatenate | solution.py:301
  23.9 0.0 copy-start.1
  23.9 0.0 copy-start.2
  23.9 2.0 %copy.13 = bf16[32,16,40,128]{3,2,1,0:T(8,128)(2,1)S(1)} copy(bf16[32,16,40,128]{3,0,2,1:T(8,128)(2,1)S(1)} %get-tuple-element.13) | data formatting | bytes 10485760 | tf_op jit(solution)/shard_map/concatenate | solution.py:301
  25.9 0.0 copy-done.1
  25.9 0.0 copy-done.2
  25.9 8.6 %templates.1 = (bf16[32,256,640]{2,1,0:T(8,128)(2,1)S(1)}, f32[1,128]{1,0:T(1,128)S(1)}) custom-call(bf16[32,640,128]{2,1,0:T(8,128)(2,1)S(1)} %bitcast.16, bf16[32,640,128]{2,1,0:T(8,128)(2,1)S(1)} %bitcast.15, f32[640,128]{1,0:T(8,128)S(1)} %bitcast.18, f32[640,128]{1,0:T(8,128)S(1)} %bitcast.17, f32[640,128]{1,0:T(8,128)S(1)} %bitcast.20, ...), custom_call_target="tpu_custom_call" | custom-call | flops 104857600 | bytes 20971520 | tf_op jit(solution)/shard_map/templates/pallas_call | solution.py:320
  34.5 0.0 copy-start
  34.5 3.9 %copy-done = bf16[32,256,640]{2,1,0:T(8,128)(2,1)} copy-done((bf16[32,256,640]{2,1,0:T(8,128)(2,1)}, bf16[32,256,640]{2,1,0:T(8,128)(2,1)S(1)}, u32[]{:S(2)}) %copy-start) | copy-done | bytes 10485784
  38.5 127.5 %gather_scan.1 = (f32[128,384]{1,0:T(8,128)}, f32[3,1,128]{2,1,0:T(1,128)}, bf16[3,32,640,128]{3,2,1,0:T(8,128)(2,1)}) custom-call(bf16[32,256,640]{2,1,0:T(8,128)(2,1)} %copy-done, bf16[256,192]{1,0:T(8,128)(2,1)} %constant.34.inverse_ref, bf16[3,32,40,128]{3,2,1,0:T(8,128)(2,1)} %bitcast.24), custom_call_target="tpu_custom_call" | custom-call | tf_op jit(solution)/shard_map/gather_scan/pallas_call | solution.py:345
  166.0 0.7 sqrt_reduce_fusion
  166.7 2.3 %fusion.5 = (f32[384]{0:T(512)}, f32[128,384]{1,0:T(8,128)}) fusion(f32[384]{0:T(512)S(1)} %bitcast.25, f32[128]{0:T(128)S(1)} %sqrt_bitcast_fusion, f32[128,384]{1,0:T(8,128)} %get-tuple-element.7), kind=kLoop, calls=%fused_computation.21 | loop fusion | flops 196224 | bytes 396800 | tf_op jit(solution)/shard_map/reduce_max | solution.py:372
  169.0 22.8 %best_of_row.1 = f32[3,128]{1,0:T(4,128)} custom-call(f32[3,128]{1,0:T(4,128)} %bitcast.26), custom_call_target="tpu_custom_call" | custom-call | tf_op jit(solution)/shard_map/best_of_row/pallas_call | solution.py:245
  191.8 1.3 copy.19
  (7 shorter events, 0.1 us)
Async XLA Ops:
  4.5 11.0 %copy-start.3 = (bf16[32,320,128]{2,1,0:T(8,128)(2,1)S(1)}, bf16[32,320,128]{2,1,0:T(8,128)(2,1)}, u32[]{:S(2)}) copy-start(bf16[32,320,128]{2,1,0:T(8,128)(2,1)} %param.12) | copy-start | bytes 7864324
  15.6 1.7 copy-start.4
  23.9 2.1 %copy-start.1 = (f32[16,40,128]{2,1,0:T(8,128)S(1)}, f32[16,40,128]{2,1,0:T(8,128)}, u32[]{:S(2)}) copy-start(f32[16,40,128]{2,1,0:T(8,128)} %pad_maximum_fusion.5) | copy-start | bytes 983044
  23.9 2.1 %copy-start.2 = (f32[16,40,128]{2,1,0:T(8,128)S(1)}, f32[16,40,128]{2,1,0:T(8,128)}, u32[]{:S(2)}) copy-start(f32[16,40,128]{2,1,0:T(8,128)} %pad_maximum_fusion.4) | copy-start | bytes 983044
  34.5 3.9 %copy-start = (bf16[32,256,640]{2,1,0:T(8,128)(2,1)}, bf16[32,256,640]{2,1,0:T(8,128)(2,1)S(1)}, u32[]{:S(2)}) copy-start(bf16[32,256,640]{2,1,0:T(8,128)(2,1)S(1)} %get-tuple-element.6.eff_ref) | copy-start | bytes 31457284

commit v2 on v1

--- a/solution.py
+++ b/solution.py
@@ -54,36 +54,9 @@
     out_ref[0] = rows[...].astype(jnp.bfloat16)
 
 
-def template_kernel(x_ref, y_ref, cos_ref, sin_ref, cos1_ref, sin1_ref, out_ref, norm_ref, cosine, sine, total):
-    f = pl.program_id(0)
-
-    @pl.when(f == 0)
-    def _():
-        cosine[...] = cos_ref[...]
-        sine[...] = sin_ref[...]
-        total[...] = jnp.zeros_like(total)
-
-    c, s = cosine[...], sine[...]
-    x = x_ref[0].astype(jnp.float32)
-    y = y_ref[0].astype(jnp.float32)
-    first = (x * c + y * s).astype(jnp.bfloat16)
-    second = (x * s - y * c).astype(jnp.bfloat16)
-    back = first.astype(jnp.float32)
-    square = back * back
-    total[...] += jnp.sum(square.reshape(square.shape[0] // 8, 8, square.shape[1]), axis=0)
-    out_ref[0] = jnp.concatenate([first, second], axis=1).T
-    c1, s1 = cos1_ref[...], sin1_ref[...]
-    cosine[...] = c * c1 - s * s1
-    sine[...] = s * c1 + c * s1
-
-    @pl.when(f == pl.num_programs(0) - 1)
-    def _():
-        norm_ref[...] = jnp.sum(total[...], axis=0, keepdims=True)
-
-
-def scan_kernel(n, pitch, count, eff_ref, inverse_ref, spec_ref, high_ref, energy_ref, gathered, buffer, cross, total, send_sem, recv_sem, own_sem, load_sem):
+def scan_kernel(n, pitch, count, x_ref, y_ref, cos_ref, sin_ref, cos1_ref, sin1_ref, inverse_ref, spec_ref, high_ref, energy_ref, norm_ref, gathered, eff_ref, cosine, sine, buffer, cross, total, send_sem, recv_sem, own_sem, load_sem):
     blocks, band, held, block = spec_ref.shape
-    templates = eff_ref.shape[1] // 2
+    templates = x_ref.shape[2]
     layers = n // 4
     me = lax.axis_index("row")
     z, y, core = me // 4, lax.rem(me // 2, 2), lax.rem(me, 2)
@@ -168,14 +141,14 @@
                 spec = buffer[f]
                 wide = spec.astype(jnp.float32)
                 square = wide * wide
-                total[...] += jnp.sum(square.reshape(square.shape[0] // 8, 8, square.shape[1]), axis=0)
+                total[:, :block] += jnp.sum(square.reshape(square.shape[0] // 8, 8, square.shape[1]), axis=0)
                 both = jnp.dot(eff_ref[f], spec, preferred_element_type=jnp.float32)
                 cross[pl.ds(f, templates, stride=pitch), :] = both[:templates]
                 cross[pl.ds(band + f, templates, stride=pitch), :] = both[templates:]
                 return carry
 
             lax.fori_loop(g * count, (g + 1) * count, one, 0)
-        energy_ref[i] = jnp.sum(total[...], axis=0, keepdims=True)
+        energy_ref[i] = jnp.sum(total[:, :block], axis=0, keepdims=True)
 
         def group(j, carry):
             found = []
@@ -197,6 +170,28 @@
             return carry
 
         lax.fori_loop(0, templates // 8, group, 0)
+
+    cosine[...] = cos_ref[...]
+    sine[...] = sin_ref[...]
+    total[...] = jnp.zeros_like(total)
+
+    def prepare(f, carry):
+        c, s = cosine[...], sine[...]
+        x = x_ref[f].astype(jnp.float32)
+        y = y_ref[f].astype(jnp.float32)
+        first = (x * c + y * s).astype(jnp.bfloat16)
+        second = (x * s - y * c).astype(jnp.bfloat16)
+        back = first.astype(jnp.float32)
+        square = back * back
+        total[:, :templates] += jnp.sum(square.reshape(square.shape[0] // 8, 8, templates), axis=0)
+        eff_ref[f] = jnp.concatenate([first, second], axis=1).T
+        c1, s1 = cos1_ref[...], sin1_ref[...]
+        cosine[...] = c * c1 - s * s1
+        sine[...] = s * c1 + c * s1
+        return carry
+
+    lax.fori_loop(0, band, prepare, 0)
+    norm_ref[...] = jnp.sum(total[:, :templates], axis=0, keepdims=True)
 
     along(0)
     over(0)
@@ -316,45 +311,26 @@
         jnp.sin(step_phase),
     ]
     tables = [rows_of(table, table) for table in tables]
-    one = pl.BlockSpec((1, depth, templates), lambda f: (f, 0, 0))
-    eff, square = pl.pallas_call(
-        template_kernel,
-        grid=(band,),
-        out_shape=(
-            jax.ShapeDtypeStruct((band, 2 * templates, depth), jnp.bfloat16),
-            jax.ShapeDtypeStruct((1, templates), jnp.float32),
-        ),
-        in_specs=[one, one, vmem, vmem, vmem, vmem],
-        out_specs=(
-            pl.BlockSpec((1, 2 * templates, depth), lambda f: (f, 0, 0)),
-            pl.BlockSpec((1, templates), lambda f: (0, 0)),
-        ),
-        scratch_shapes=[
-            pltpu.VMEM((depth, templates), jnp.float32),
-            pltpu.VMEM((depth, templates), jnp.float32),
-            pltpu.VMEM((8, templates), jnp.float32),
-        ],
-        compiler_params=pltpu.CompilerParams(vmem_limit_bytes=32 * 1024 * 1024),
-        cost_estimate=pl.CostEstimate(flops=40 * band * depth * templates, bytes_accessed=8 * band * depth * templates, transcendentals=0),
-        name="templates",
-    )(x, y, *tables)
-
     count = math.gcd(band, 4)
     pitch = 2 * band + 8
     anywhere = pl.BlockSpec(memory_space=pl.ANY)
-    highest, energy, _ = pl.pallas_call(
+    highest, energy, square, _ = pl.pallas_call(
         functools.partial(scan_kernel, n, pitch, count),
         out_shape=(
             jax.ShapeDtypeStruct((templates, windows), jnp.float32),
             jax.ShapeDtypeStruct((blocks, 1, block), jnp.float32),
+            jax.ShapeDtypeStruct((1, templates), jnp.float32),
             jax.ShapeDtypeStruct((blocks, band, depth, block), jnp.bfloat16),
         ),
-        in_specs=[vmem, vmem, anywhere],
-        out_specs=(vmem, vmem, anywhere),
+        in_specs=[vmem] * 7 + [anywhere],
+        out_specs=(vmem, vmem, vmem, anywhere),
         scratch_shapes=[
+            pltpu.VMEM((band, 2 * templates, depth), jnp.bfloat16),
+            pltpu.VMEM((depth, templates), jnp.float32),
+            pltpu.VMEM((depth, templates), jnp.float32),
             pltpu.VMEM((band, depth, block), jnp.bfloat16),
             pltpu.VMEM((templates * pitch, block), jnp.float32),
-            pltpu.VMEM((8, block), jnp.float32),
+            pltpu.VMEM((8, max(block, templates)), jnp.float32),
             pltpu.SemaphoreType.DMA((3 * n, blocks)),
             pltpu.SemaphoreType.DMA((blocks, n)),
             pltpu.SemaphoreType.DMA((blocks,)),
@@ -364,7 +340,7 @@
             collective_id=1, has_side_effects=True, vmem_limit_bytes=VMEM_LIMIT
         ),
         name="gather_scan",
-    )(eff, inverse3, spectra)
+    )(x, y, *tables, inverse3, spectra)
     data_norm = jnp.sqrt(energy.reshape(1, windows) + epsilon)
     templ_norm = jnp.sqrt(square + epsilon).reshape(templates, 1)
     scale = math.sqrt(2.0 * channels * band)

time: 193 us -> 188 us (0.974)
  Pallas kernels: 170 us -> 162 us
  other arithmetic: 11.3 us -> 13.4 us
    pallas_call x1 -> x0, Pallas kernels: 8.59 us -> none  [body(): pl.pallas_call(template_kernel, grid=(band,), out_shape=(jax.ShapeDtypeSt...]
    concatenate x2, local copies, waits for them, and re-layouts: 4.05 us -> 8.61 us  [rows_of(): jnp.concatenate([first.reshape(shape), second.reshape(shape)], axis=-2)]
    unnamed x12 -> x6, local copies, waits for them, and re-layouts: 6.93 us -> 2.97 us
where the time goes in v2:
time: 188 us
  Pallas kernels  162 us (86%)
  other arithmetic  13.4 us (7%)
  local copies, waits for them, and re-layouts  11.6 us (6%)
    pallas_call x1, Pallas kernels, body(): pl.pallas_call(functools.partial(scan_kernel, n, pitch, count), out_shape...  128 us
    pallas_call x1, Pallas kernels, best_of_row(): pl.pallas_call(functools.partial(best_kernel, n), out_shape=jax.ShapeDtyp...  22.9 us
    pallas_call x1, Pallas kernels, body(): pl.pallas_call(front_kernel, grid=(blocks,), out_shape=jax.ShapeDtypeStru...  11 us
    concatenate x2, local copies, waits for them, and re-layouts, rows_of(): jnp.concatenate([first.reshape(shape), second.reshape(shape)], axis=-2)  8.61 us
    concatenate x5, other arithmetic, rows_of(): jnp.concatenate([first.reshape(shape), second.reshape(shape)], axis=-2)  5.63 us

profile of v2, /device:TPU:0, one launch (start us, length us, event | category | flops | bytes accessed | tf_op | source)
XLA Modules:
  0.0 187.6 jit_solution(13005805262871010712)
XLA Ops:
  0.6 2.3 %sine_multiply_fusion = (f32[320,128]{1,0:T(8,128)S(1)}, f32[320,128]{1,0:T(8,128)S(1)}, f32[320,128]{1,0:T(8,128)S(1)}, f32[320,128]{1,0:T(8,128)S(1)}) fusion(s32[320,128]{1,0:T(8,128)} %param.13, s32[320,128]{1,0:T(8,128)} %param.14), kind=kLoop, calls=%fused_computation.14 | loop fusion | flops 778240 | bytes 983040 | tf_op jit(solution)/shard_map/mul | solution.py:309
  2.9 0.8 pad_maximum_fusion.3
  3.7 0.8 pad_maximum_fusion.2
  4.5 0.8 pad_maximum_fusion.5
  5.3 0.8 pad_maximum_fusion.4
  6.0 0.0 copy-start
  6.0 11.0 %front.1 = bf16[3,1280,128]{2,1,0:T(8,128)(2,1)} custom-call(f32[32]{0:T(128)} %taps_ref.1, f32[256,64]{1,0:T(8,128)} %constant.30.clone.forward_ref, f32[20,384,512]{2,1,0:T(8,128)} %raw_ref.1), custom_call_target="tpu_custom_call" | custom-call | tf_op jit(solution)/shard_map/front/pallas_call | solution.py:275
  17.0 0.0 copy-start.1
  17.0 0.0 copy-done
  17.1 1.7 copy.12
  18.7 0.0 copy-done.1
  18.8 1.9 %copy_negate_fusion = (bf16[32,320,128]{2,0,1:T(8,128)(2,1)S(1)}, bf16[32,320,128]{2,0,1:T(8,128)(2,1)S(1)}) fusion(bf16[32,320,128]{2,1,0:T(8,128)(2,1)S(1)} %copy-done.1), kind=kLoop, calls=%fused_computation.20 | loop fusion | flops 1310720 | bytes 7864320 | tf_op jit(solution)/shard_map/neg | solution.py:302
  20.7 2.6 %pad_maximum_fusion.1 = (bf16[32,16,40,128]{3,0,2,1:T(8,128)(2,1)S(1)}, bf16[32,16,40,128]{3,0,2,1:T(8,128)(2,1)S(1)}) fusion(bf16[32,16,20,128]{3,0,2,1:T(8,128)(2,1)S(1)} %bitcast.18, bf16[32,16,20,128]{3,0,2,1:T(8,128)(2,1)S(1)} %bitcast.17, bf16[32,16,20,128]{3,0,2,1:T(8,128)(2,1)S(1)} %bitcast.19), kind=kLoop, calls=%fused_computation.1 | loop fusion | flops 5242880 | bytes 18350080 | tf_op jit(solution)/shard_map/concatenate | solution.py:296
  23.3 4.3 %copy.15 = bf16[32,16,40,128]{3,2,1,0:T(8,128)(2,1)} copy(bf16[32,16,40,128]{3,0,2,1:T(8,128)(2,1)S(1)} %get-tuple-element.10) | data formatting | bytes 10485760 | tf_op jit(solution)/shard_map/concatenate | solution.py:296
  27.6 4.3 %copy.13 = bf16[32,16,40,128]{3,2,1,0:T(8,128)(2,1)} copy(bf16[32,16,40,128]{3,0,2,1:T(8,128)(2,1)S(1)} %get-tuple-element.11) | data formatting | bytes 10485760 | tf_op jit(solution)/shard_map/concatenate | solution.py:296
  31.9 127.9 %gather_scan.1 = (f32[128,384]{1,0:T(8,128)}, f32[3,1,128]{2,1,0:T(1,128)}, f32[1,128]{1,0:T(1,128)}, bf16[3,32,640,128]{3,2,1,0:T(8,128)(2,1)}) custom-call(bf16[32,640,128]{2,1,0:T(8,128)(2,1)} %bitcast.16, bf16[32,640,128]{2,1,0:T(8,128)(2,1)} %bitcast.15, f32[640,128]{1,0:T(8,128)} %bitcast.22, f32[640,128]{1,0:T(8,128)} %bitcast.21, ...), custom_call_target="tpu_custom_call" | custom-call | tf_op jit(solution)/shard_map/gather_scan/pallas_call | solution.py:317
  159.8 0.6 sqrt_bitcast_fusion
  160.4 0.7 sqrt_reduce_fusion
  161.1 2.3 %fusion.5 = (f32[384]{0:T(512)}, f32[128,384]{1,0:T(8,128)}) fusion(f32[384]{0:T(512)S(1)} %bitcast.25, f32[128]{0:T(128)S(1)} %sqrt_bitcast_fusion, f32[128,384]{1,0:T(8,128)} %get-tuple-element.5), kind=kLoop, calls=%fused_computation.21 | loop fusion | flops 196224 | bytes 396800 | tf_op jit(solution)/shard_map/reduce_max | solution.py:348
  163.4 22.9 %best_of_row.1 = f32[3,128]{1,0:T(4,128)} custom-call(f32[3,128]{1,0:T(4,128)} %bitcast.26), custom_call_target="tpu_custom_call" | custom-call | tf_op jit(solution)/shard_map/best_of_row/pallas_call | solution.py:240
  186.3 1.2 copy.19
  (4 shorter events, 0.1 us)
Async XLA Ops:
  6.0 11.0 %copy-start = (bf16[32,320,128]{2,1,0:T(8,128)(2,1)S(1)}, bf16[32,320,128]{2,1,0:T(8,128)(2,1)}, u32[]{:S(2)}) copy-start(bf16[32,320,128]{2,1,0:T(8,128)(2,1)} %param.12) | copy-start | bytes 7864324
  17.0 1.7 copy-start.1
